TPU v7x, 512 devices: a whole 4x4x16 slice. The times are simulated.
512 devices in a mesh: dp: 64 (over x, z_lo, core), mp: 8 (over y, z_hi).
Axes of the slice: x: 4, y: 4, z: 16 (z_hi: 2, z_lo: 8; z = z_hi * 8 + z_lo), core: 2. Of those that a mesh axis runs over, the one named last changes fastest.
Arguments:
- master: float32 [8, 256, 512], P('mp', 'dp'), may hold values from -4 to 4
- moment: float32 [8, 256, 512], P('mp', 'dp'), may hold values from -0.06 to 0.06
- variance: float32 [8, 256, 512], P('mp', 'dp'), may hold values from 3e-06 to 3e-05
- flat_slot: int32 [256], replicated, may hold values from 0 to 255, each once
- feedback: bfloat16 [64, 2, 64, 8192], P('dp', None, 'mp'), may hold values from -0.029907227 to 0.029907227
- activations: bfloat16 [2, 8192, 8192], P(None, ('dp', 'mp')), may hold values from -24 to 24
- output_grads: bfloat16 [2, 8192, 8192], P(None, ('dp', 'mp')), may hold values from -24 to 24
Outputs:
- master_out: float32 [8, 256, 512], P('mp', 'dp')
- moment_out: float32 [8, 256, 512], P('mp', 'dp')
- feedback_out: bfloat16 [64, 2, 64, 8192], P('dp', None, 'mp')
Inputs may be any that keep to these rules, and one draw needn't show every extreme that they name: `flat_slot`: every position of the flat buffer holds exactly one of the 256 segments.
All inputs are finite; a program needn't handle non-finite values. Where the computation divides by a largest or mean magnitude, that divisor is 1e-20 or more.
Results may differ from a plain program's by a relative error of at most 0.0036.
The roundings to bfloat16 on the way count: a program that leaves them out, or rounds other values in their place, can miss the bound.
Values may be sent and summed in bfloat16 or wider, within the bound.
A program may use at most 64 MiB of HBM per device.

v0:
```python
import jax
import jax.numpy as jnp
from jax import lax
from jax.sharding import PartitionSpec as P

beta_one = 0.9
step_rate = 0.05
epsilon = 1e-08
down_scale = 28672.0 ** (-0.5)


def silu_slope(preact):
    sigmoid_value = jax.nn.sigmoid(preact)
    return sigmoid_value * (1.0 + preact * (1.0 - sigmoid_value))


def gradients(weights, inputs, cotangent, model_width):
    up_scale = model_width ** (-0.5)
    before = up_scale * jnp.dot(inputs, weights[0].T, preferred_element_type=jnp.float32)
    hidden = jax.nn.silu(before).astype(jnp.bfloat16)
    back_grad = down_scale * jnp.dot(cotangent, weights[1].T, preferred_element_type=jnp.float32)
    slope_grad = (back_grad * silu_slope(before)).astype(jnp.bfloat16)
    grad_up = up_scale * jnp.dot(slope_grad.T, inputs, preferred_element_type=jnp.float32)
    grad_down = down_scale * jnp.dot(hidden.T, cotangent, preferred_element_type=jnp.float32)
    return jnp.stack([grad_up, grad_down])


def per_device(master, moment, variance, flat_slot, feedback, activations, output_grads):
    owner_rows = master.shape[1]
    total_rows = flat_slot.shape[0]
    hidden_rows = feedback.shape[2]
    model_width = feedback.shape[3]
    workers = lax.axis_size("dp")
    tensor_shape = (2, hidden_rows, model_width)
    segment_shape = (total_rows, master.shape[2])
    inverse = (
        jnp.zeros((total_rows,), jnp.int32)
        .at[flat_slot]
        .set(jnp.arange(total_rows, dtype=jnp.int32))
    )
    working_flat = lax.all_gather(master[0].astype(jnp.bfloat16), "dp", axis=0, tiled=True)
    moment_flat, variance_flat = (
        lax.all_gather(moment[0], "dp", axis=0, tiled=True),
        lax.all_gather(variance[0], "dp", axis=0, tiled=True),
    )
    working = working_flat[flat_slot].reshape(tensor_shape)
    moment_t = moment_flat[flat_slot].reshape(tensor_shape)
    denominator = jnp.sqrt(variance_flat[flat_slot].reshape(tensor_shape)) + epsilon
    group_inputs, group_grads = (
        lax.all_gather(activations, "mp", axis=1, tiled=True),
        lax.all_gather(output_grads, "mp", axis=1, tiled=True),
    )
    step_one = gradients(working, group_inputs[0], group_grads[0], model_width)
    local_moment = beta_one * moment_t + (1.0 - beta_one) * step_one
    local_weights = (working.astype(jnp.float32) - step_rate * local_moment / denominator).astype(
        jnp.bfloat16
    )
    step_two = gradients(local_weights, group_inputs[1], group_grads[1], model_width)
    shifted = local_moment + feedback[0].astype(jnp.float32)
    magnitude = jnp.mean(jnp.abs(shifted), axis=-1, keepdims=True) + 1e-06
    packed = magnitude * jnp.tanh(shifted / magnitude)
    new_error = (shifted - packed).astype(jnp.bfloat16)
    first_row = lax.axis_index("dp") * owner_rows
    grad_flat = step_two.reshape(segment_shape)[inverse]
    moment_whole = lax.psum(packed, "dp")
    own_segments = lax.dynamic_slice_in_dim(inverse, first_row, owner_rows, 0)
    moment_own = moment_whole.reshape(segment_shape)[own_segments]
    grad_own = lax.psum_scatter(grad_flat, "dp", scatter_dimension=0, tiled=True)
    mean_moment = moment_own / workers
    mean_grad = grad_own / workers
    moment_new = beta_one * mean_moment + (1.0 - beta_one) * mean_grad
    owner_denominator = jnp.sqrt(variance[0]) + epsilon
    master_new = master[0] - step_rate * (mean_moment + moment_new) / owner_denominator
    return (master_new[None], moment_new[None], new_error[None])


def solution(mesh):
    in_specs = (
        P("mp", "dp", None),
        P("mp", "dp", None),
        P("mp", "dp", None),
        P(),
        P("dp", None, "mp", None),
        P(None, ("dp", "mp"), None),
        P(None, ("dp", "mp"), None),
    )
    out_specs = (P("mp", "dp", None), P("mp", "dp", None), P("dp", None, "mp", None))
    return jax.shard_map(
        per_device, mesh=mesh, in_specs=in_specs, out_specs=out_specs, check_vma=False
    )
```

profile of v0, /device:TPU:1, one launch (start us, length us, event | category | flops | bytes accessed | tf_op | source)
XLA Modules:
  0.0 1362.9 jit_solution(14703939547487024372)
XLA Ops:
  7.2 0.0 all-gather.8.cloned.1.call-start
  7.2 0.7 all-gather.8.cloned.1.call-update
  7.9 0.0 all-gather.6.cloned.1.call-start
  7.9 0.7 all-gather.6.cloned.1.call-update
  8.6 0.0 all-reduce.4.cloned.1.call-start
  8.7 0.7 copy.10
  9.4 181.0 %all-gather = f32[1,256,512]{2,0,1:T(1,128)S(1)} all-gather(f32[1,4,512]{2,0,1:T(1,128)S(1)} %copy.10), channel_id=2, replica_groups=mesh['dp'=64,'mp'=8] {'dp'}, dimensions={1}, use_global_device_ids=true | all-gather | bytes 532480 | tf_op jit(solution)/shard_map/all_gather | solution.py:43
  190.5 0.0 copy-start.2
  190.5 0.7 compare_select_fusion.1
  191.2 1.0 gather_fusion
  192.1 0.0 copy-start.3
  192.1 0.1 broadcast_multiply_fusion
  192.2 0.1 mul.139
  192.3 0.1 mul.173
  192.4 0.0 copy-done.2
  192.4 172.0 %all-gather.2 = bf16[64,4,512]{2,1,0:T(4,128)(2,1)S(1)} all-gather(bf16[1,4,512]{2,1,0:T(4,128)(2,1)S(1)} %fusion.24), channel_id=1, replica_groups=mesh['dp'=64,'mp'=8] {'dp'}, dimensions={0}, use_global_device_ids=true | all-gather | bytes 266240 | tf_op jit(solution)/shard_map/all_gather | solution.py:41
  364.4 0.1 reshape.144
  364.5 1.2 gather_fusion.1
  365.6 0.1 reshape.83
  365.8 0.0 copy-done.3
  365.8 114.9 %all-gather.1 = f32[1,256,512]{2,0,1:T(1,128)S(1)} all-gather(f32[1,4,512]{2,0,1:T(1,128)S(1)} %copy.11), channel_id=3, replica_groups=mesh['dp'=64,'mp'=8] {'dp'}, dimensions={1}, use_global_device_ids=true | all-gather | bytes 532480 | tf_op jit(solution)/shard_map/all_gather | solution.py:44
  480.7 1.0 gather_fusion.3
  481.7 0.1 sqrt_add_fusion
  481.8 0.1 add.91
  481.9 0.1 squeeze.40
  482.0 0.1 squeeze.38
  482.1 1.4 scatter_custom_fusion
  483.5 1.3 dynamic-slice
  485.4 0.1 compare_select_fusion.2
  485.5 0.0 copy-start
  485.5 0.0 all-gather.8.cloned.1.call-done
  485.6 2.3 fusion.12
  487.8 2.0 convolution_multiply_fusion.2
  489.8 3.8 convolution_multiply_fusion.3
  493.6 0.0 copy-done
  493.6 0.2 abs_reduce_fusion
  493.8 0.9 subtract_convert_fusion.1
  494.8 0.9 reshape.80
  495.7 2.3 fusion.7
  498.0 2.0 fusion
  500.0 3.8 fusion.1
  503.8 0.1 reshape.81
  503.9 1.8 gather_fusion.4
  505.8 0.0 all-reduce.4.cloned.1.call-update
  505.8 0.9 subtract_convert_fusion
  506.6 846.8 %all-reduce.4.cloned.1.call-done = (f32[256,512]{1,0:T(8,128)}, f32[256,512]{1,0:T(8,128)}) async-done(((f32[256,512]{1,0:T(8,128)}, f32[256,512]{1,0:T(8,128)}), (f32[256,512]{1,0:T(8,128)}, f32[256,512]{1,0:T(8,128)})) %all-reduce.4.cloned.1.call-update) | async-done | bytes 1048592 | tf_op jit(solution)/shard_map/psum | solution.py:65
  1353.5 1.6 gather_fusion.2
  1355.1 1.3 fusion.33
  (15 shorter events, 0.2 us)
Async XLA Ops:
  7.2 478.4 %all-gather.8.cloned.1.call-start = ((), (), s32[]{:S(2)}) async-start(), calls=%async_computation.1 | async-start | bytes 4718592 | tf_op jit(solution)/shard_map/all_gather | solution.py:50
  7.9 480.0 %all-gather.6.cloned.1.call-start = ((), (), s32[]{:S(2)}) async-start(), calls=%async_computation | async-start | bytes 4718592 | tf_op jit(solution)/shard_map/all_gather | solution.py:51
  8.6 1344.8 %all-reduce.4.cloned.1.call-start = ((), (), s32[]{:S(2)}) async-start(), calls=%async_computation.2 | async-start | bytes 2097152 | tf_op jit(solution)/shard_map/psum | solution.py:65
  190.5 2.0 copy-start.2
  192.1 173.6 %copy-start.3 = (f32[1,4,512]{2,1,0:T(4,128)S(1)}, f32[1,4,512]{2,1,0:T(4,128)}, u32[]{:S(2)}) copy-start(f32[1,4,512]{2,1,0:T(4,128)} %param.9) | copy-start | bytes 24580
  485.5 8.1 copy-start
  494.8 5.2 copy-start.1
Sparse Core Ops, SparseCore 0:
  11.2 185.7 all-gather.7
  200.2 170.1 all-gather.5
  505.9 847.5 all-reduce.3
where the time goes:
time: 1360 us
  waiting for transfers between devices  848 us (62%)
  blocking collectives  468 us (34%)
  matrix products  16.1 us (1%)
  between operations  14.6 us (1%)
    psum x1, waiting for transfers between devices, per_device(): moment_whole = lax.psum(packed, 'dp')  847 us
    all_gather x1, blocking collectives, per_device(): lax.all_gather(moment[0], 'dp', axis=0, tiled=True)  181 us
    all_gather x1, blocking collectives, per_device(): lax.all_gather(master[0].astype(jnp.bfloat16), 'dp', axis=0, tiled=True)  172 us
    all_gather x1, blocking collectives, per_device(): lax.all_gather(variance[0], 'dp', axis=0, tiled=True)  115 us
  transfers between devices with their start and end apart: 3, of which 1 were waited for; matrix products, arithmetic and copies ran while one was open for 1% of the time, Pallas kernels for 0%

commit v1 on v0

--- a/solution.py
+++ b/solution.py
@@ -38,7 +38,11 @@
         .at[flat_slot]
         .set(jnp.arange(total_rows, dtype=jnp.int32))
     )
-    working_flat = lax.all_gather(master[0].astype(jnp.bfloat16), "dp", axis=0, tiled=True)
+    direct_views = lambda row_data, along_axis: jnp.concatenate(
+        lax.all_to_all(jnp.stack([row_data] * lax.axis_size(along_axis), axis=0), along_axis, 0, 0),
+        axis=0,
+    )
+    working_flat = direct_views(master[0].astype(jnp.bfloat16), "dp")
     moment_flat, variance_flat = (
         lax.all_gather(moment[0], "dp", axis=0, tiled=True),
         lax.all_gather(variance[0], "dp", axis=0, tiled=True),

time: 1360 us -> 1260 us (0.926)
  blocking collectives: 468 us -> 341 us
  starting transfers between devices: 0.11 us -> 17.2 us
    all_gather x1 -> x0, blocking collectives: 172 us -> none  [per_device(): lax.all_gather(master[0].astype(jnp.bfloat16), 'dp', axis=0, tiled=True)]
    all_gather x1, blocking collectives: 115 us -> 174 us  [per_device(): lax.all_gather(variance[0], 'dp', axis=0, tiled=True)]
    all_to_all x0 -> x1, starting transfers between devices: none -> 17 us  [per_device(): lax.all_to_all(jnp.stack([row_data] * lax.axis_size(along_axis), axis=0),...]
  transfers between devices with their start and end apart: 3 -> 4, of which waited for: 1 -> 1; matrix products, arithmetic and copies ran while one was open for 1% -> 1% of each run, Pallas kernels for 0% -> 0%
where the time goes in v1:
time: 1260 us
  waiting for transfers between devices  848 us (67%)
  blocking collectives  341 us (27%)
  starting transfers between devices  17.2 us (1%)
  matrix products  16.1 us (1%)
  between operations  14.6 us (1%)
    psum x1, waiting for transfers between devices, per_device(): moment_whole = lax.psum(packed, 'dp')  847 us
    all_gather x1, blocking collectives, per_device(): lax.all_gather(variance[0], 'dp', axis=0, tiled=True)  174 us
    all_gather x1, blocking collectives, per_device(): lax.all_gather(moment[0], 'dp', axis=0, tiled=True)  167 us
  transfers between devices with their start and end apart: 4, of which 1 were waited for; matrix products, arithmetic and copies ran while one was open for 1% of the time, Pallas kernels for 0%

profile of v1, /device:TPU:1, one launch (start us, length us, event | category | flops | bytes accessed | tf_op | source)
XLA Modules:
  0.0 1255.2 jit_solution(12530627213712996668)
XLA Ops:
  7.2 0.0 all-gather.7.cloned.1.call-start
  7.2 0.7 all-gather.7.cloned.1.call-update
  7.9 0.0 all-gather.5.cloned.1.call-start
  7.9 0.7 all-gather.5.cloned.1.call-update
  8.6 0.7 convert_bitcast_fusion.1
  9.3 0.8 stack.23
  10.1 17.0 %all-to-all-start = ((bf16[64,4,512]{2,1,0:T(4,128)(2,1)}), bf16[64,4,512]{2,1,0:T(4,128)(2,1)S(1)}, u32[]{:S(2)}, u32[]{:S(2)}) async-start(bf16[64,4,512]{2,1,0:T(4,128)(2,1)} %stack.23), calls=%async_computation | async-start | bytes 524288 | tf_op jit(solution)/shard_map/all_to_all | solution.py:42
  27.2 0.0 all-reduce.4.cloned.1.call-start
  27.2 0.7 copy.10
  27.9 167.4 %all-gather = f32[1,256,512]{2,0,1:T(1,128)S(1)} all-gather(f32[1,4,512]{2,0,1:T(1,128)S(1)} %copy.10), channel_id=2, replica_groups=mesh['dp'=64,'mp'=8] {'dp'}, dimensions={1}, use_global_device_ids=true | all-gather | bytes 532480 | tf_op jit(solution)/shard_map/all_gather | solution.py:47
  195.4 0.0 copy-start.3
  195.4 0.7 compare_select_fusion.1
  196.1 1.0 gather_fusion
  197.1 0.1 broadcast_multiply_fusion
  197.1 0.1 mul.139
  197.2 0.1 mul.173
  197.4 174.0 %all-gather.1 = f32[1,256,512]{2,0,1:T(1,128)S(1)} all-gather(f32[1,4,512]{2,0,1:T(1,128)S(1)} %copy.11), channel_id=3, replica_groups=mesh['dp'=64,'mp'=8] {'dp'}, dimensions={1}, use_global_device_ids=true | all-gather | bytes 532480 | tf_op jit(solution)/shard_map/all_gather | solution.py:48
  371.4 1.0 gather_fusion.3
  372.4 0.1 sqrt_add_fusion
  372.6 0.1 add.91
  372.7 1.4 scatter_custom_fusion
  374.1 1.3 dynamic-slice
  376.0 0.1 compare_select_fusion.2
  376.1 0.0 all-to-all-done
  376.1 0.1 reshape.84
  376.2 1.2 gather_fusion.1
  377.4 0.1 reshape.88
  377.5 0.1 squeeze.40
  377.6 0.1 squeeze.38
  377.6 0.0 copy-start
  377.6 0.0 all-gather.7.cloned.1.call-done
  377.7 2.3 fusion.12
  379.9 2.0 convolution_multiply_fusion.2
  381.9 3.8 convolution_multiply_fusion.3
  385.7 0.2 abs_reduce_fusion
  385.9 0.9 subtract_convert_fusion.1
  386.9 0.9 reshape.85
  387.8 2.3 fusion.7
  390.1 2.0 fusion
  392.1 3.8 fusion.1
  395.9 0.0 copy-start.2
  395.9 0.1 reshape.86
  396.0 1.8 gather_fusion.4
  397.8 0.0 all-reduce.4.cloned.1.call-update
  397.8 0.9 subtract_convert_fusion
  398.7 847.0 %all-reduce.4.cloned.1.call-done = (f32[256,512]{1,0:T(8,128)}, f32[256,512]{1,0:T(8,128)}) async-done(((f32[256,512]{1,0:T(8,128)}, f32[256,512]{1,0:T(8,128)}), (f32[256,512]{1,0:T(8,128)}, f32[256,512]{1,0:T(8,128)})) %all-reduce.4.cloned.1.call-update) | async-done | bytes 1048592 | tf_op jit(solution)/shard_map/psum | solution.py:69
  1245.7 1.6 gather_fusion.2
  1247.3 1.3 fusion.32
  (17 shorter events, 0.2 us)
Async XLA Ops:
  7.2 370.5 %all-gather.7.cloned.1.call-start = ((), (), s32[]{:S(2)}) async-start(), calls=%async_computation.2 | async-start | bytes 4718592 | tf_op jit(solution)/shard_map/all_gather | solution.py:54
  7.9 372.1 %all-gather.5.cloned.1.call-start = ((), (), s32[]{:S(2)}) async-start(), calls=%async_computation.1 | async-start | bytes 4718592 | tf_op jit(solution)/shard_map/all_gather | solution.py:55
  10.1 366.0 %all-to-all-start = ((bf16[64,4,512]{2,1,0:T(4,128)(2,1)}), bf16[64,4,512]{2,1,0:T(4,128)(2,1)S(1)}, u32[]{:S(2)}, u32[]{:S(2)}) async-start(bf16[64,4,512]{2,1,0:T(4,128)(2,1)} %stack.23), calls=%async_computation | async-start | bytes 524288 | tf_op jit(solution)/shard_map/all_to_all | solution.py:42
  27.2 1218.5 %all-reduce.4.cloned.1.call-start = ((), (), s32[]{:S(2)}) async-start(), calls=%async_computation.3 | async-start | bytes 2097152 | tf_op jit(solution)/shard_map/psum | solution.py:69
  195.4 2.0 copy-start.3
  377.6 8.1 copy-start
  386.9 5.2 copy-start.1
  395.9 851.4 %copy-start.2 = (f32[1,4,512]{2,1,0:T(4,128)S(1)}, f32[1,4,512]{2,1,0:T(4,128)}, u32[]{:S(2)}) copy-start(f32[1,4,512]{2,1,0:T(4,128)} %param.7) | copy-start | bytes 24580
Sparse Core Ops, SparseCore 0:
  11.2 188.6 all-gather.6
  203.1 171.2 all-gather.4
  398.0 847.7 all-reduce.3

commit v2 on v0

--- a/solution.py
+++ b/solution.py
@@ -62,7 +62,8 @@
     new_error = (shifted - packed).astype(jnp.bfloat16)
     first_row = lax.axis_index("dp") * owner_rows
     grad_flat = step_two.reshape(segment_shape)[inverse]
-    moment_whole = lax.psum(packed, "dp")
+    parts = lax.all_gather(packed, "dp", axis=0, tiled=False)
+    moment_whole = parts.sum(axis=0)
     own_segments = lax.dynamic_slice_in_dim(inverse, first_row, owner_rows, 0)
     moment_own = moment_whole.reshape(segment_shape)[own_segments]
     grad_own = lax.psum_scatter(grad_flat, "dp", scatter_dimension=0, tiled=True)

time: 1360 us -> 1550 us (1.14)
  waiting for transfers between devices: 848 us -> 1020 us
    psum x1 -> x0, waiting for transfers between devices: 847 us -> none  [per_device(): moment_whole = lax.psum(packed, 'dp')]
    unnamed x3 -> x5, waiting for transfers between devices: 1.39 us -> 826 us
    all_gather x0 -> x1, waiting for transfers between devices: none -> 194 us  [per_device(): parts = lax.all_gather(packed, 'dp', axis=0, tiled=False)]
  transfers between devices with their start and end apart: 3 -> 4, of which waited for: 1 -> 2; matrix products, arithmetic and copies ran while one was open for 1% -> 2% of each run, Pallas kernels for 0% -> 0%
where the time goes in v2:
time: 1550 us; the launch traced here: 1540 us
  waiting for transfers between devices  1020 us (66%)
  blocking collectives  469 us (30%)
  matrix products  16.1 us (1%)
    unnamed x5, waiting for transfers between devices  826 us
    all_gather x1, waiting for transfers between devices, per_device(): parts = lax.all_gather(packed, 'dp', axis=0, tiled=False)  194 us
    all_gather x1, blocking collectives, per_device(): lax.all_gather(moment[0], 'dp', axis=0, tiled=True)  183 us
    all_gather x1, blocking collectives, per_device(): lax.all_gather(master[0].astype(jnp.bfloat16), 'dp', axis=0, tiled=True)  171 us
    all_gather x1, blocking collectives, per_device(): lax.all_gather(variance[0], 'dp', axis=0, tiled=True)  115 us
  transfers between devices with their start and end apart: 4, of which 2 were waited for; matrix products, arithmetic and copies ran while one was open for 2% of the time, Pallas kernels for 0%

profile of v2, /device:TPU:1, one launch (start us, length us, event | category | flops | bytes accessed | tf_op | source)
XLA Modules:
  0.0 1544.7 jit_solution(12941746847995815206)
XLA Ops:
  7.2 0.0 all-gather.9.cloned.1.call-start
  7.2 0.7 all-gather.9.cloned.1.call-update
  7.9 0.0 all-gather.7.cloned.1.call-start
  7.9 0.7 all-gather.7.cloned.1.call-update
  8.6 0.0 all-gather.11.cloned.1.call-start
  8.7 0.7 copy.10
  9.4 183.4 %all-gather = f32[1,256,512]{2,0,1:T(1,128)S(1)} all-gather(f32[1,4,512]{2,0,1:T(1,128)S(1)} %copy.10), channel_id=2, replica_groups=mesh['dp'=64,'mp'=8] {'dp'}, dimensions={1}, use_global_device_ids=true | all-gather | bytes 532480 | tf_op jit(solution)/shard_map/all_gather | solution.py:43
  192.9 0.0 copy-start.1
  192.9 0.7 compare_select_fusion.1
  193.6 1.0 gather_fusion
  194.6 0.0 copy-start.2
  194.6 0.1 broadcast_multiply_fusion
  194.6 0.1 mul.138
  194.7 0.1 mul.152
  194.9 171.0 %all-gather.2 = bf16[64,4,512]{2,1,0:T(4,128)(2,1)S(1)} all-gather(bf16[1,4,512]{2,1,0:T(4,128)(2,1)S(1)} %fusion.26), channel_id=1, replica_groups=mesh['dp'=64,'mp'=8] {'dp'}, dimensions={0}, use_global_device_ids=true | all-gather | bytes 266240 | tf_op jit(solution)/shard_map/all_gather | solution.py:41
  365.8 0.1 reshape.149
  365.9 1.2 gather_fusion.1
  367.1 0.1 reshape.88
  367.2 0.1 squeeze.40
  367.3 0.1 squeeze.38
  367.4 114.7 %all-gather.1 = f32[1,256,512]{2,0,1:T(1,128)S(1)} all-gather(f32[1,4,512]{2,0,1:T(1,128)S(1)} %copy.11), channel_id=3, replica_groups=mesh['dp'=64,'mp'=8] {'dp'}, dimensions={1}, use_global_device_ids=true | all-gather | bytes 532480 | tf_op jit(solution)/shard_map/all_gather | solution.py:44
  482.1 1.0 gather_fusion.3
  483.1 0.1 sqrt_add_fusion
  483.2 0.1 add.93
  483.3 0.0 copy-start
  483.3 0.0 all-gather.9.cloned.1.call-done
  483.3 2.3 fusion.12
  485.6 2.0 convolution_multiply_fusion.2
  487.6 3.8 convolution_multiply_fusion.3
  491.4 0.2 subtract_convert_fusion.1
  491.6 1.0 subtract_convert_fusion
  492.7 0.0 all-gather.11.cloned.1.call-update
  492.7 0.0 all-reduce.3.cloned.1.call-start
  492.8 1.4 scatter_custom_fusion
  494.2 2.2 fusion.7
  496.4 2.0 fusion
  498.4 3.8 fusion.1
  502.2 0.1 reshape.86
  502.3 1.8 gather_fusion.4
  504.1 0.0 all-reduce.3.cloned.1.call-update
  504.2 1.3 dynamic-slice
  506.1 0.1 compare_select_fusion.2
  506.2 193.9 %all-gather.11.cloned.1.call-done = f32[64,2,8,8192]{3,2,1,0:T(8,128)} async-done(((f32[1,2,8,8192]{3,2,1,0:T(8,128)}), f32[64,2,8,8192]{3,2,1,0:T(8,128)}) %all-gather.11.cloned.1.call-update) | async-done | bytes 33554448 | tf_op jit(solution)/shard_map/all_gather | solution.py:65
  700.1 11.7 reduce_sum.19
  711.7 0.1 reshape.85
  711.8 0.6 gather_fusion.2
  712.4 824.4 %all-reduce.3.cloned.1.call-done = f32[256,512]{1,0:T(8,128)} async-done(((f32[256,512]{1,0:T(8,128)}), f32[256,512]{1,0:T(8,128)}) %all-reduce.3.cloned.1.call-update) | async-done | bytes 524304
  1536.8 1.3 fusion.35
  (16 shorter events, 0.2 us)
Async XLA Ops:
  7.2 476.2 %all-gather.9.cloned.1.call-start = ((), (), s32[]{:S(2)}) async-start(), calls=%async_computation.1 | async-start | bytes 4718592 | tf_op jit(solution)/shard_map/all_gather | solution.py:50
  7.9 477.7 %all-gather.7.cloned.1.call-start = ((), (), s32[]{:S(2)}) async-start(), calls=%async_computation | async-start | bytes 4718592 | tf_op jit(solution)/shard_map/all_gather | solution.py:51
  8.6 691.4 %all-gather.11.cloned.1.call-start = ((), (), s32[]{:S(2)}) async-start(), calls=%async_computation.2 | async-start | bytes 34078720 | tf_op jit(solution)/shard_map/all_gather | solution.py:65
  192.9 2.0 copy-start.1
  194.6 172.8 %copy-start.2 = (f32[1,4,512]{2,1,0:T(4,128)S(1)}, f32[1,4,512]{2,1,0:T(4,128)}, u32[]{:S(2)}) copy-start(f32[1,4,512]{2,1,0:T(4,128)} %param.9) | copy-start | bytes 24580
  483.3 8.1 copy-start
  492.7 1044.1 %all-reduce.3.cloned.1.call-start = ((), (), s32[]{:S(2)}) async-start(), calls=%async_computation.3 | async-start | bytes 1048576
Sparse Core Ops, SparseCore 0:
  11.2 185.2 all-gather.8
  199.7 170.8 all-gather.6
  492.8 207.1 all-gather.10
  702.8 833.9 all-reduce.2
